TPU v7x, 32 devices: a whole 2x2x4 slice. The times are simulated.
32 devices in a mesh: parts: 2 (over x), virt: 16 (over z, y, core).
Axes of the slice: x: 2, y: 2, z: 4, core: 2. Of those that a mesh axis runs over, the one named last changes fastest.
Arguments:
- trials: float32 [4096, 4, 256], P(('parts', 'virt')), parts along dimension 0, may hold values from -6 to 6
- vv_vectors: float32 [48, 2048, 2048], P('parts', 'virt'), parts along dimension 0, may hold values from -0.125 to 0.125
- oo_vectors: float32 [48, 256, 256], P('parts'), parts along dimension 0, may hold values from -0.078125 to 0.078125
- occ_energy: float32 [512], P('parts'), parts along dimension 0, may hold values from -2 to -0.5
- virt_energy: float32 [4096], P(('parts', 'virt')), parts along dimension 0, may hold values from 0.5 to 5, as said below
Outputs:
- filtered: float32 [4096, 4, 256], P(('parts', 'virt')), parts along dimension 0
- gram: float32 [8, 4], P('parts'), parts along dimension 0
There are 2 independent parts, one for each index of `parts`. A program takes and returns all parts, laid end to end along the dimension named above; each array names one. Nothing has to cross between parts.
Inputs may be any that keep to these rules, and one draw needn't show every extreme that they name: `virt_energy`: rises with the orbital index, with a rough jitter.
All inputs are finite; a program needn't handle non-finite values.
Results may differ from a plain program's by a relative error of at most 0.0001.
Values sent between devices are 32-bit elements; how exact they have to be, the bound alone decides.
A program may use at most 128 MiB of HBM per device.

v0:
```python
import functools

import jax
import jax.numpy as jnp
from jax import lax
from jax.experimental import pallas as pl
from jax.experimental.pallas import tpu as pltpu
from jax.sharding import PartitionSpec as P

AHEAD_Y = 4
AHEAD_C = 2
STAGES = 8
ROW_TILE = 768


def halves(x):
    high = x.astype(jnp.bfloat16)
    low = (x - high.astype(jnp.float32)).astype(jnp.bfloat16)
    return high, low


def kernel(sizes, trials, vv, oo, gap, out, gram, vh, vl, oh, ol, yh, yl, slots, acc,
           vstage, ostage, tile, tiles, v_sem, o_sem, own_sem, sz, sy, sc, rz, ry, rc, sg, rg, og):
    n, lines, across, count, rows, width, vectors, group = sizes
    groups = 2 * count
    steps = groups * lines
    me = lax.axis_index("virt")
    core = lax.rem(me, 2)
    chip = me // 2
    my_b = lax.rem(chip, across)
    my_a = chip // across
    partner = me + 1 - 2 * core

    def place(b, c):
        return pl.ds(pl.multiple_of((b * 2 + c) * rows, rows), rows)

    def device(a, b, c):
        return {"virt": (a * across + b) * 2 + c}

    barrier = pltpu.get_barrier_semaphore()

    def greet(s, carry):
        pl.semaphore_signal(barrier, inc=1, device_id={"virt": lax.rem(me + s, n)})
        return carry

    def v_copy(q):
        i, p = q // vectors, lax.rem(q, vectors)
        a = lax.rem(my_a + i, lines)
        slot = lax.rem(q, STAGES)
        return pltpu.make_async_copy(
            vv.at[p, :, pl.ds(pl.multiple_of(a * group, group), group)],
            vstage.at[slot], v_sem.at[slot])

    def o_copy(p):
        slot = lax.rem(p, 4)
        return pltpu.make_async_copy(oo.at[p], ostage.at[slot], o_sem.at[slot])

    for q in range(STAGES):
        v_copy(jnp.int32(q)).start()
    for p in range(4):
        o_copy(jnp.int32(p)).start()
    lax.fori_loop(1, n, greet, 0)
    pl.semaphore_wait(barrier, n - 1)

    def z_send(g, src):
        for j in range(1, lines):
            a = lax.rem(my_a + j, lines)
            pltpu.make_async_remote_copy(
                src_ref=src, dst_ref=slots.at[g, my_a, place(my_b, core)],
                send_sem=sz.at[g], recv_sem=rz.at[g, my_a],
                device_id=device(a, my_b, core)).start()

    def wait_bytes(amount, sem):
        ref = slots.at[0, 0, pl.ds(0, amount)]
        pltpu.make_async_copy(ref, ref, sem).wait()

    def y_forward(s):
        g, i = s // lines, lax.rem(s, lines)
        a = lax.rem(my_a + i, lines)

        @pl.when(i != 0)
        def _():
            wait_bytes(rows, rz.at[g, a])

        mine = slots.at[g, a, place(my_b, core)]
        for j in range(1, across):
            pltpu.make_async_remote_copy(
                src_ref=mine, dst_ref=mine, send_sem=sy.at[g], recv_sem=ry.at[g, a],
                device_id=device(my_a, lax.rem(my_b + j, across), core)).start()

    def c_forward(s):
        g, i = s // lines, lax.rem(s, lines)
        a = lax.rem(my_a + i, lines)
        wait_bytes((across - 1) * rows, ry.at[g, a])
        for b in range(across):
            block = slots.at[g, a, place(b, core)]
            pltpu.make_async_remote_copy(
                src_ref=block, dst_ref=block, send_sem=sc.at[g], recv_sem=rc.at[g, a],
                device_id={"virt": partner}).start()

    own = [
        pltpu.make_async_copy(
            trials.at[k], slots.at[k, my_a, place(my_b, core)], own_sem.at[k])
        for k in range(count)
    ]
    for k in range(count):
        own[k].start()
    for k in range(count):
        z_send(k, trials.at[k])
    for k in range(count):
        own[k].wait()
    y_forward(jnp.int32(0))

    def split_oo(p, carry):
        o_copy(p).wait()
        high, low = halves(ostage[lax.rem(p, 4)])
        oh[p] = high
        ol[p] = low

        @pl.when(p + 4 < vectors)
        def _():
            o_copy(p + 4).start()
        return carry

    lax.fori_loop(0, vectors, split_oo, 0)
    for s in range(1, AHEAD_Y):
        y_forward(jnp.int32(s))
        if s <= AHEAD_C:
            c_forward(jnp.int32(s - 1))

    def step(s, carry):
        g, i = s // lines, lax.rem(s, lines)
        a = lax.rem(my_a + i, lines)

        @pl.when(s + AHEAD_Y < steps)
        def _():
            y_forward(s + AHEAD_Y)

        @pl.when(s + AHEAD_C < steps)
        def _():
            c_forward(s + AHEAD_C)

        @pl.when(g == 0)
        def _():
            def split_vv(p, inner):
                q = i * vectors + p
                v_copy(q).wait()
                high, low = halves(vstage[lax.rem(q, STAGES)])
                where = pl.ds(pl.multiple_of(p * rows, rows), rows)
                vh[a, where] = high
                vl[a, where] = low

                @pl.when(q + STAGES < lines * vectors)
                def _():
                    v_copy(q + STAGES).start()
                return inner

            lax.fori_loop(0, vectors, split_vv, 0)

        wait_bytes(across * rows, rc.at[g, a])
        high, low = halves(slots[g, a])
        yh[...] = high
        yl[...] = low
        total_rows = vectors * rows
        tall = min(ROW_TILE, total_rows)

        def product(t, inner):
            where = pl.ds(pl.multiple_of(t * tall, tall), tall)
            top, rest = vh[a, where], vl[a, where]
            left = jnp.concatenate([top, top, rest], axis=1)
            right = jnp.concatenate([yh[...], yl[...], yh[...]], axis=0)
            term = jnp.dot(left, right, preferred_element_type=jnp.float32)
            acc[where] = jnp.where(i == 0, term, acc[where] + term)
            return inner

        lax.fori_loop(0, total_rows // tall, product, 0)

        @pl.when(i == lines - 1)
        def _():
            def second(p, running):
                zh, zl = halves(acc[pl.ds(pl.multiple_of(p * rows, rows), rows)])
                left = jnp.concatenate([zh, zh, zl], axis=1)
                right = jnp.concatenate([oh[p], ol[p], oh[p]], axis=0)
                return running + jnp.dot(left, right, preferred_element_type=jnp.float32)

            direct = lax.fori_loop(
                0, vectors, second, jnp.zeros((rows, width), jnp.float32), unroll=2)

            @pl.when(g < count)
            def _():
                y = trials[g]
                mine = slots.at[g + count, my_a, place(my_b, core)]
                mine[...] = ((gap[...] * y - direct) - 4.5 * y) / 3.0
                z_send(g + count, mine)

            @pl.when(g >= count)
            def _():
                y = slots[g, my_a, place(my_b, core)]
                out[g - count] = 2.0 * ((gap[...] * y - direct) - 4.5 * y) / 3.0 - trials[g - count]

        return carry

    lax.fori_loop(0, steps, step, 0)

    row = lax.broadcasted_iota(jnp.int32, tile.shape, 0)
    col = lax.broadcasted_iota(jnp.int32, tile.shape, 1)
    part = jnp.zeros(tile.shape, jnp.float32)
    for k in range(count):
        for l in range(k, count):
            value = jnp.sum(out[k] * out[l])
            hit = ((row == k) & (col == l)) | ((row == l) & (col == k))
            part = jnp.where(hit, value, part)
    tile[...] = part
    tiles[me] = part

    def send(s, carry):
        pltpu.make_async_remote_copy(
            src_ref=tile, dst_ref=tiles.at[me], send_sem=sg, recv_sem=rg,
            device_id={"virt": lax.rem(me + s, n)}).start()
        return carry

    lax.fori_loop(1, n, send, 0)
    for g in range(groups):
        wait_bytes((lines - 1) * rows, sz.at[g])
        for _ in range(across - 1):
            wait_bytes(lines * rows, sy.at[g])
        for _ in range(across):
            wait_bytes(lines * rows, sc.at[g])
    others = tiles.at[pl.ds(0, n - 1)]
    pltpu.make_async_copy(others, others, rg).wait()
    gram[...] = jnp.sum(tiles[...], axis=0) / (n * rows * width)
    pltpu.make_async_copy(others, others, sg).wait()


def per_device(trials, vv_vectors, oo_vectors, occ_energy, virt_energy):
    n = lax.axis_size("virt")
    rows, count, width = trials.shape
    vectors = vv_vectors.shape[0]
    chips = n // 2
    across = 1
    while across * across * 4 <= chips:
        across *= 2
    across = max(across, 2)
    lines = chips // across
    group = across * 2 * rows
    gap = virt_energy[:, None] - occ_energy[None, :]
    sizes = (n, lines, across, count, rows, width, vectors, group)
    groups = 2 * count
    f32, bf16 = jnp.float32, jnp.bfloat16
    dma = pltpu.SemaphoreType.DMA
    vmem = pl.BlockSpec(memory_space=pltpu.VMEM)
    hbm = pl.BlockSpec(memory_space=pl.ANY)
    out, gram = pl.pallas_call(
        functools.partial(kernel, sizes),
        out_shape=(
            jax.ShapeDtypeStruct((count, rows, width), f32),
            jax.ShapeDtypeStruct((8, 128), f32),
        ),
        in_specs=[vmem, hbm, hbm, vmem],
        out_specs=(vmem, vmem),
        scratch_shapes=[
            pltpu.VMEM((lines, vectors * rows, group), bf16),
            pltpu.VMEM((lines, vectors * rows, group), bf16),
            pltpu.VMEM((vectors, width, width), bf16),
            pltpu.VMEM((vectors, width, width), bf16),
            pltpu.VMEM((group, width), bf16),
            pltpu.VMEM((group, width), bf16),
            pltpu.VMEM((groups, lines, group, width), f32),
            pltpu.VMEM((vectors * rows, width), f32),
            pltpu.VMEM((STAGES, rows, group), f32),
            pltpu.VMEM((4, width, width), f32),
            pltpu.VMEM((8, 128), f32),
            pltpu.VMEM((n, 8, 128), f32),
            dma((STAGES,)), dma((4,)), dma((count,)),
            dma((groups,)), dma((groups,)), dma((groups,)),
            dma((groups, lines)), dma((groups, lines)), dma((groups, lines)),
            dma, dma, dma,
        ],
        compiler_params=pltpu.CompilerParams(
            collective_id=0, has_side_effects=True, vmem_limit_bytes=63 * 2**20),
        name="filter_step",
    )(jnp.transpose(trials, (1, 0, 2)), vv_vectors, oo_vectors, gap)
    return (jnp.transpose(out, (1, 0, 2)), gram[:count, :count])


def solution(mesh):
    in_specs = (
        P(("parts", "virt"), None, None),
        P("parts", "virt", None),
        P("parts", None, None),
        P("parts"),
        P(("parts", "virt")),
    )
    out_specs = (P(("parts", "virt"), None, None), P("parts", None))
    return jax.shard_map(
        per_device, mesh=mesh, in_specs=in_specs, out_specs=out_specs, check_vma=False
    )
```

profile of v0, /device:TPU:0, one launch (start us, length us, event | category | flops | bytes accessed | tf_op | source)
XLA Modules:
  0.0 191.8 jit_solution(10722921779836344238)
XLA Ops:
  0.6 1.4 broadcast_subtract_fusion.gap
  2.0 1.9 %copy.10 = f32[128,4,256]{2,0,1:T(8,128)} copy(f32[128,4,256]{2,1,0:T(4,128)} %param.5) | data formatting | bytes 1048576 | tf_op args[0]
  4.0 184.4 %filter_step.1 = (f32[4,128,256]{2,1,0:T(8,128)}, f32[8,128]{1,0:T(8,128)}) custom-call(f32[4,128,256]{2,1,0:T(8,128)} %bitcast.4, f32[24,128,2048]{2,1,0:T(8,128)} %vv.1, f32[24,256,256]{2,1,0:T(8,128)} %oo.1, f32[128,256]{1,0:T(8,128)} %broadcast_subtract_fusion.gap), custom_call_target="tpu_custom_call" | custom-call | tf_op jit(solution)/shard_map/filter_step/pallas_call | solution.py:253
  188.3 2.2 %copy.8 = f32[128,4,256]{2,1,0:T(4,128)} copy(f32[128,4,256]{2,0,1:T(8,128)} %bitcast.5) | data formatting | bytes 1048576
  190.5 1.3 slice.3
where the time goes:
time: 192 us
  Pallas kernels  184 us (96%)
  local copies, waits for them, and re-layouts  5.37 us (3%)
    pallas_call x1, Pallas kernels, per_device(): pl.pallas_call(functools.partial(kernel, sizes), out_shape=(jax.ShapeDtyp...  184 us
    unnamed x2, local copies, waits for them, and re-layouts  4.11 us

commit v1 on v0

--- a/solution.py
+++ b/solution.py
@@ -11,6 +11,7 @@
 AHEAD_C = 2
 STAGES = 8
 ROW_TILE = 768
+TOGETHER = 8
 
 
 def halves(x):
@@ -164,27 +165,29 @@
         total_rows = vectors * rows
         tall = min(ROW_TILE, total_rows)
 
-        def product(t, inner):
-            where = pl.ds(pl.multiple_of(t * tall, tall), tall)
+        for t in range(total_rows // tall):
+            where = pl.ds(t * tall, tall)
             top, rest = vh[a, where], vl[a, where]
             left = jnp.concatenate([top, top, rest], axis=1)
             right = jnp.concatenate([yh[...], yl[...], yh[...]], axis=0)
             term = jnp.dot(left, right, preferred_element_type=jnp.float32)
             acc[where] = jnp.where(i == 0, term, acc[where] + term)
-            return inner
-
-        lax.fori_loop(0, total_rows // tall, product, 0)
 
         @pl.when(i == lines - 1)
         def _():
-            def second(p, running):
-                zh, zl = halves(acc[pl.ds(pl.multiple_of(p * rows, rows), rows)])
-                left = jnp.concatenate([zh, zh, zl], axis=1)
-                right = jnp.concatenate([oh[p], ol[p], oh[p]], axis=0)
-                return running + jnp.dot(left, right, preferred_element_type=jnp.float32)
+            def second(q, running):
+                left, right = [], []
+                for u in range(TOGETHER):
+                    p = q * TOGETHER + u
+                    zh, zl = halves(acc[pl.ds(pl.multiple_of(p * rows, rows), rows)])
+                    left += [zh, zh, zl]
+                    right += [oh[p], ol[p], oh[p]]
+                return running + jnp.dot(
+                    jnp.concatenate(left, axis=1), jnp.concatenate(right, axis=0),
+                    preferred_element_type=jnp.float32)
 
             direct = lax.fori_loop(
-                0, vectors, second, jnp.zeros((rows, width), jnp.float32), unroll=2)
+                0, vectors // TOGETHER, second, jnp.zeros((rows, width), jnp.float32))
 
             @pl.when(g < count)
             def _():

time: 192 us -> 161 us (0.84)
  Pallas kernels: 184 us -> 153 us
    pallas_call x1, Pallas kernels: 184 us -> 153 us  [per_device(): pl.pallas_call(functools.partial(kernel, sizes), out_shape=(jax.ShapeDtyp...]
where the time goes in v1:
time: 161 us; the launch traced here: 160 us
  Pallas kernels  153 us (95%)
  local copies, waits for them, and re-layouts  5.37 us (3%)
    pallas_call x1, Pallas kernels, per_device(): pl.pallas_call(functools.partial(kernel, sizes), out_shape=(jax.ShapeDtyp...  153 us
    unnamed x2, local copies, waits for them, and re-layouts  4.11 us

profile of v1, /device:TPU:0, one launch (start us, length us, event | category | flops | bytes accessed | tf_op | source)
XLA Modules:
  0.0 160.1 jit_solution(11570441461695492129)
XLA Ops:
  0.6 1.4 broadcast_subtract_fusion.gap
  2.0 1.9 %copy.10 = f32[128,4,256]{2,0,1:T(8,128)} copy(f32[128,4,256]{2,1,0:T(4,128)} %param.5) | data formatting | bytes 1048576 | tf_op args[0]
  4.0 152.6 %filter_step.1 = (f32[4,128,256]{2,1,0:T(8,128)}, f32[8,128]{1,0:T(8,128)}) custom-call(f32[4,128,256]{2,1,0:T(8,128)} %bitcast.4, f32[24,128,2048]{2,1,0:T(8,128)} %vv.1, f32[24,256,256]{2,1,0:T(8,128)} %oo.1, f32[128,256]{1,0:T(8,128)} %broadcast_subtract_fusion.gap), custom_call_target="tpu_custom_call" | custom-call | tf_op jit(solution)/shard_map/filter_step/pallas_call | solution.py:256
  156.6 2.2 %copy.8 = f32[128,4,256]{2,1,0:T(4,128)} copy(f32[128,4,256]{2,0,1:T(8,128)} %bitcast.5) | data formatting | bytes 1048576
  158.8 1.3 slice.3
